TPU v7x, 128 devices: a whole 4x4x4 slice. The times are simulated.
128 devices in a mesh: leaf: 4 (over x_lo, core), row: 8 (over x_hi, y), col: 4 (over z).
Axes of the slice: x: 4 (x_hi: 2, x_lo: 2; x = x_hi * 2 + x_lo), y: 4, z: 4, core: 2. Of those that a mesh axis runs over, the one named last changes fastest.
Arguments:
- parent_adj: float32 [16384, 16384], P(('leaf', 'row'), 'col'), may hold values from -70 to 70, as said below
- child_map: int32 [4, 8], replicated, may hold values from 0 to 127, as said below
- lower_panel: float32 [4, 1024, 4096], P('leaf', 'col', 'row'), may hold values from -0.09375 to 0.09375
- pivot_inverse: float32 [4, 4096, 4096], P('leaf', 'row', 'col'), may hold values from -1 to 3, as said below
Outputs:
- update_adj: float32 [4, 1024, 1024], P('leaf', 'row', 'col')
- off_adj: float32 [4, 1024, 4096], P('leaf', 'row', 'col')
- pivot_adj: float32 [4, 4096, 4096], P('leaf', 'row', 'col')
Inputs may be any that keep to these rules, and one draw needn't show every extreme that they name: `child_map`: each row lists 8 distinct parent block ids in increasing order; every row contains block 0 and block 127. parent_adj is symmetric. Each pivot_inverse[c] is lower triangular with diagonal entries of 1 to 3.
All inputs are finite; a program needn't handle non-finite values.
Results may differ from a plain program's by a relative error of at most 0.0003.
Values sent between devices are 32-bit elements; how exact they have to be, the bound alone decides.
A program may use at most 128 MiB of HBM per device.

v0:
```python
import jax
import jax.numpy as jnp
from jax import lax
from jax.sharding import PartitionSpec as P

BLK = 128


exact_mode = lax.Precision.HIGHEST


def take_child(blocks_view, block_ids):
    return jnp.take(blocks_view, block_ids, axis=0)


def shards(parent_adj, child_map, lower_panel, pivot_inverse):
    row_count = lax.axis_size("row")
    column_count = lax.axis_size("col")
    leaf_index = lax.axis_index("leaf")
    row_index = lax.axis_index("row")
    column_index = lax.axis_index("col")
    children = child_map.shape[0]
    blocks_all = child_map.shape[1]
    local_rows = parent_adj.shape[0]
    local_columns = parent_adj.shape[1]
    row_blocks = local_rows // BLK
    column_blocks = local_columns // BLK
    per_column = blocks_all // column_count
    per_row = blocks_all // row_count
    width = per_column * BLK
    column_ids = jnp.transpose(child_map.reshape(children, column_count, per_column), (1, 0, 2))
    column_local = column_ids - column_index * column_blocks
    column_owned = (column_local >= 0) & (column_local < column_blocks)
    column_safe = jnp.clip(column_local, 0, column_blocks - 1)
    parent_view = parent_adj.reshape(local_rows, column_blocks, BLK)
    picked = jnp.take(parent_view, column_safe.reshape(-1), axis=1)
    picked = picked.reshape(local_rows, column_count, children, per_column, BLK)
    picked = jnp.where(column_owned[None, :, :, :, None], picked, 0.0)
    picked = picked.reshape(local_rows, column_count, children * width)
    columns_kept = lax.psum_scatter(picked, "col", scatter_dimension=1, tiled=True)
    selected = columns_kept.reshape(row_blocks, BLK, children, width)
    by_child = jnp.moveaxis(selected, 2, 0)
    owner = leaf_index * row_count + row_index
    row_local = child_map - owner * row_blocks
    row_owned = (row_local >= 0) & (row_local < row_blocks)
    row_safe = jnp.clip(row_local, 0, row_blocks - 1)
    contribution = jax.vmap(take_child)(by_child, row_safe)
    contribution = jnp.where(row_owned[:, :, None, None], contribution, 0.0)
    update = lax.psum_scatter(
        contribution.reshape(children * row_count * per_row * BLK, width),
        ("leaf", "row"),
        scatter_dimension=0,
        tiled=True,
    )
    lower = lower_panel[0]
    inverse = pivot_inverse[0]
    lower_all = lax.all_gather(lower, "col", axis=0, tiled=True)
    factor = lax.psum_scatter(
        jnp.dot(lower_all, inverse, precision=exact_mode, preferred_element_type=jnp.float32),
        "row",
        scatter_dimension=0,
        tiled=True,
    )
    update_all = lax.all_gather(update, "col", axis=1, tiled=True)
    carried = jnp.dot(
        update_all,
        lax.all_gather(factor, "row", axis=0, tiled=True),
        precision=exact_mode,
        preferred_element_type=jnp.float32,
    )
    factor_all, inverse_all = (
        lax.all_gather(factor, "col", axis=1, tiled=True),
        lax.all_gather(inverse, "col", axis=1, tiled=True),
    )
    first = jnp.dot(factor_all.T, carried, precision=exact_mode, preferred_element_type=jnp.float32)
    second = jnp.dot(
        inverse_all.T, inverse, precision=exact_mode, preferred_element_type=jnp.float32
    )
    pivot = lax.psum_scatter(first + second, "row", scatter_dimension=0, tiled=True)
    return (update[None], (-2.0 * carried)[None], pivot[None])


def solution(mesh):
    in_specs = (P(("leaf", "row"), "col"), P(), P("leaf", "col", "row"), P("leaf", "row", "col"))
    out_specs = (P("leaf", "row", "col"), P("leaf", "row", "col"), P("leaf", "row", "col"))
    return jax.shard_map(shards, mesh=mesh, in_specs=in_specs, out_specs=out_specs, check_vma=False)
```

profile of v0, /device:TPU:32, one launch (start us, length us, event | category | flops | bytes accessed | tf_op | source)
XLA Modules:
  0.0 789.2 jit_solution(10354824878462700312)
XLA Ops:
  7.2 0.7 all-gather.11.cloned.1.call-update
  7.9 0.7 subtract_clamp_fusion
  8.7 0.1 copy.43
  8.8 0.1 copy.41
  9.1 0.7 compare_and_fusion.3
  10.0 9.0 %copy.42 = f32[512,4096]{0,1:T(8,128)} copy(f32[512,4096]{1,0:T(8,128)} %param.4) | data formatting | bytes 16777216 | tf_op args[0]
  19.0 9.0 %copy.44 = f32[512,32,128]{2,0,1:T(8,128)} copy(f32[512,32,128]{0,2,1:T(8,128)} %bitcast.49) | data formatting | bytes 16777216 | tf_op jit(solution)/shard_map/reshape | solution.py:35
  28.1 0.1 reshape.79
  28.2 7.8 gather_fusion
  36.0 9.0 %copy.45 = f32[512,32,128]{0,2,1:T(8,128)} copy(f32[512,32,128]{2,0,1:T(8,128)} %bitcast.47) | data formatting | bytes 16777216 | tf_op jit(solution)/shard_map/jit(_take)/gather | solution.py:36
  45.0 7.4 fusion.2
  52.5 1.5 copy-done
  54.0 9.7 %fusion.5 = f32[1024,1024]{1,0:T(8,128)} fusion(f32[1,512,1024]{2,1,0:T(8,128)S(1)} %copy-done, f32[1,1024,512]{2,1,0:T(8,128)} %all-gather.11.cloned.1.call-done), kind=kOutput, calls=%fused_computation.10 | convolution fusion | flops 6442450944 | bytes 8388608 | tf_op jit(solution)/shard_map/dot_general | solution.py:59
  63.8 0.5 all-gather.13.cloned.1.call-update
  64.6 69.4 %reduce-scatter.5.cloned.1.call-done = f32[512,1,1024]{0,2,1:T(8,128)} async-done(((f32[512,4,1024]{0,2,1:T(8,128)}), f32[512,1,1024]{0,2,1:T(8,128)}) %reduce-scatter.5.cloned.1.call-update) | async-done | bytes 2097168 | tf_op jit(solution)/shard_map/reduce_scatter | solution.py:40
  134.0 2.9 reshape.103
  136.9 1.9 copy.47
  138.8 2.8 gather_fusion.1
  141.5 6.7 fusion.3
  148.4 74.9 %reduce-scatter.9.cloned.1.call-done = f32[128,1024]{1,0:T(8,128)} async-done(((f32[1024,1024]{1,0:T(8,128)}), f32[128,1024]{1,0:T(8,128)}) %reduce-scatter.9.cloned.1.call-update) | async-done | bytes 524304 | tf_op jit(solution)/shard_map/reduce_scatter | solution.py:58
  223.3 0.7 all-gather.9.cloned.1.call-update
  224.1 0.2 reduce-scatter.11.cloned.1.call-start
  224.3 82.7 %all-gather.13.cloned.1.call-done = f32[1,512,4096]{2,1,0:T(8,128)} async-done(((f32[1,512,1024]{2,1,0:T(8,128)}), f32[1,512,4096]{2,1,0:T(8,128)}) %all-gather.13.cloned.1.call-update) | async-done | bytes 8388624 | tf_op jit(solution)/shard_map/all_gather | solution.py:73
  307.0 30.7 %fusion = f32[4096,1024]{1,0:T(8,128)} fusion(f32[1,512,4096]{2,1,0:T(8,128)} %all-gather.13.cloned.1.call-done, f32[1,512,1024]{2,1,0:T(8,128)S(1)} %copy-done.1), kind=kOutput, calls=%fused_computation.3 | convolution fusion | flops 25769803776 | bytes 27262976 | tf_op jit(solution)/shard_map/dot_general | solution.py:76
  337.6 125.0 %reduce-scatter.7.cloned.1.call-done = f32[128,256]{1,0:T(8,128)} async-done(((f32[4096,256]{1,0:T(8,128)}), f32[128,256]{1,0:T(8,128)}) %reduce-scatter.7.cloned.1.call-update) | async-done | bytes 131088 | tf_op jit(solution)/shard_map/reduce_scatter | solution.py:49
  462.7 14.5 %all_gather.15 = f32[128,1024]{1,0:T(8,128)S(1)} all-gather(f32[128,256]{1,0:T(8,128)} %reduce-scatter.7.cloned.1.call-done), channel_id=1, replica_groups=mesh['leaf'=4,'row'=8,'col'=4] {'col'}, dimensions={1}, use_global_device_ids=true | all-gather | bytes 655360 | tf_op jit(solution)/shard_map/all_gather | solution.py:64
  477.2 63.6 %all-gather.7.cloned.1.call-done = f32[1024,1024]{1,0:T(8,128)} async-done(((f32[128,1024]{1,0:T(8,128)}), f32[1024,1024]{1,0:T(8,128)}) %all-gather.7.cloned.1.call-update) | async-done | bytes 4194320 | tf_op jit(solution)/shard_map/all_gather | solution.py:67
  540.8 4.6 fusion.9
  545.4 25.1 %all-gather.9.cloned.1.call-done = f32[128,4096]{1,0:T(8,128)} async-done(((f32[128,1024]{1,0:T(8,128)}), f32[128,4096]{1,0:T(8,128)}) %all-gather.9.cloned.1.call-update) | async-done | bytes 2097168 | tf_op jit(solution)/shard_map/all_gather | solution.py:72
  570.4 19.1 %convolution_add_fusion = f32[4096,1024]{1,0:T(8,128)} fusion(f32[4096,1024]{1,0:T(8,128)} %fusion, f32[128,4096]{1,0:T(8,128)} %all-gather.9.cloned.1.call-done, f32[128,1024]{1,0:T(8,128)S(1)} %fusion.9), kind=kOutput, calls=%fused_computation.2 | convolution fusion | flops 6446645248 | bytes 36175872 | tf_op jit(solution)/shard_map/dot_general | solution.py:75
  589.6 0.8 multiply_bitcast_fusion
  590.4 192.0 %reduce-scatter.11.cloned.1.call-done = f32[512,1024]{1,0:T(8,128)} async-done(((f32[4096,1024]{1,0:T(8,128)}), f32[512,1024]{1,0:T(8,128)}) %reduce-scatter.11.cloned.1.call-update) | async-done | bytes 2097168 | tf_op jit(solution)/shard_map/reduce_scatter | solution.py:79
  (31 shorter events, 1.0 us)
Async XLA Ops:
  7.2 45.3 %all-gather.11.cloned.1.call-start = ((), (), s32[]{:S(2)}) async-start(), calls=%async_computation.10 | async-start | bytes 2621440 | tf_op jit(solution)/shard_map/all_gather | solution.py:57
  7.9 126.1 %reduce-scatter.5.cloned.1.call-start = ((), (), s32[]{:S(2)}) async-start(), calls=%async_computation.4 | async-start | bytes 10485760 | tf_op jit(solution)/shard_map/reduce_scatter | solution.py:40
  52.4 1.6 copy-start
  52.4 170.8 %reduce-scatter.9.cloned.1.call-start = ((), (), s32[]{:S(2)}) async-start(), calls=%async_computation.6 | async-start | bytes 4718592 | tf_op jit(solution)/shard_map/reduce_scatter | solution.py:58
  63.7 0.7 copy-start.2
  63.7 243.2 %all-gather.13.cloned.1.call-start = ((), (), s32[]{:S(2)}) async-start(), calls=%async_computation.11 | async-start | bytes 10485760 | tf_op jit(solution)/shard_map/all_gather | solution.py:73
  64.3 398.3 %reduce-scatter.7.cloned.1.call-start = ((), (), s32[]{:S(2)}) async-start(), calls=%async_computation.5 | async-start | bytes 4325376 | tf_op jit(solution)/shard_map/reduce_scatter | solution.py:49
  148.3 158.7 %copy-start.1 = (f32[1,512,1024]{2,1,0:T(8,128)S(1)}, f32[1,512,1024]{2,1,0:T(8,128)}, u32[]{:S(2)}) copy-start(f32[1,512,1024]{2,1,0:T(8,128)} %param.7) | copy-start | bytes 6291460
  148.3 392.5 %all-gather.7.cloned.1.call-start = ((), (), s32[]{:S(2)}) async-start(), calls=%async_computation.7 | async-start | bytes 4718592 | tf_op jit(solution)/shard_map/all_gather | solution.py:67
  223.3 347.1 %all-gather.9.cloned.1.call-start = ((), (), s32[]{:S(2)}) async-start(), calls=%async_computation.8 | async-start | bytes 2621440 | tf_op jit(solution)/shard_map/all_gather | solution.py:72
  224.1 558.3 %reduce-scatter.11.cloned.1.call-start = ((), (), s32[]{:S(2)}) async-start(), calls=%async_computation.9 | async-start | bytes 18874368 | tf_op jit(solution)/shard_map/reduce_scatter | solution.py:79
Sparse Core Ops, SparseCore 0:
  9.7 31.9 all-gather.10
  52.6 81.3 reduce-scatter.4
  137.8 85.4 reduce-scatter.8
  224.9 82.0 all-gather.12
  309.9 152.7 reduce-scatter.6
  465.1 75.5 all-gather.6
  542.5 27.8 all-gather.8
  589.7 192.6 reduce-scatter.10
where the time goes:
time: 791 us; the launch traced here: 789 us
  waiting for transfers between devices  635 us (80%)
  matrix products  64 us (8%)
  local copies, waits for them, and re-layouts  44.8 us (6%)
  other arithmetic  16.4 us (2%)
  blocking collectives  14.5 us (2%)
  between operations  14.2 us (2%)
    reduce_scatter x1, waiting for transfers between devices, shards(): lax.psum_scatter(first + second, 'row', scatter_dimension=0, tiled=True)  192 us
    reduce_scatter x1, waiting for transfers between devices, shards(): lax.psum_scatter(contribution.reshape(children * row_count * per_row * BL...  125 us
    all_gather x1, waiting for transfers between devices, shards(): lax.all_gather(inverse, 'col', axis=1, tiled=True)  82.7 us
    reduce_scatter x1, waiting for transfers between devices, shards(): lax.psum_scatter(jnp.dot(lower_all, inverse, precision=exact_mode, prefer...  74.9 us
    reduce_scatter x1, waiting for transfers between devices, shards(): lax.psum_scatter(picked, 'col', scatter_dimension=1, tiled=True)  69.4 us
    all_gather x1, waiting for transfers between devices, shards(): lax.all_gather(factor, 'row', axis=0, tiled=True)  63.6 us
    dot_general x1, matrix products, shards(): jnp.dot(inverse_all.T, inverse, precision=exact_mode, preferred_element_t...  30.7 us
    all_gather x1, waiting for transfers between devices, shards(): lax.all_gather(factor, 'col', axis=1, tiled=True)  25.1 us
  transfers between devices with their start and end apart: 8, of which 7 were waited for; matrix products, arithmetic and copies ran while one was open for 13% of the time, Pallas kernels for 0%

commit v1 on v0

v1 whole, which is shorter than its diff:
```python
import jax
import jax.numpy as jnp
from jax import lax
from jax.experimental import pallas as pl
from jax.experimental.pallas import tpu as pltpu
from jax.sharding import PartitionSpec as P

BLK = 128
MESH = pl.DeviceIdType.MESH
F32 = jnp.float32
BF16 = jnp.bfloat16


def split(a):
    high = a.astype(BF16)
    return high, (a - high.astype(F32)).astype(BF16)


def dot3(a_high, a_low, b_high, b_low):
    dot = lambda p, q: jnp.dot(p, q, preferred_element_type=F32)
    return dot(a_high, b_high) + (dot(a_high, b_low) + dot(a_low, b_high))


def place():
    leaf, row, col = lax.axis_index("leaf"), lax.axis_index("row"), lax.axis_index("col")
    return leaf, leaf // 2, leaf % 2, row, row // 4, row % 4, col


def neighbours():
    leaf, xl, _, row, h, y, z = place()
    return dict(
        zp=(leaf, row, (z + 1) % 4),
        zm=(leaf, row, (z + 3) % 4),
        yp=(leaf, h * 4 + (y + 1) % 4, z),
        ym=(leaf, h * 4 + (y + 3) % 4, z),
        xp=((leaf + 2) % 4, (row + 4 * xl) % 8, z),
        xm=((leaf + 2) % 4, (row + 4 * (1 - xl)) % 8, z),
        hx=(leaf, (row + 4) % 8, z),
        core=(xl * 2 + (1 - leaf % 2), row, z),
    )


class Copies:
    def __init__(self, send, recv):
        self.send, self.recv, self.count = send, recv, 0

    def make(self, src, dst, device):
        n = self.count
        self.count += 1
        return pltpu.make_async_remote_copy(
            src_ref=src, dst_ref=dst, send_sem=self.send.at[n], recv_sem=self.recv.at[n], device_id=device, device_id_type=MESH
        )


class Scatter:
    def __init__(self, copies, x, first, second, pos, plus, minus, add):
        self.x, self.first, self.second, self.pos, self.add = x, first, second, pos, add
        self.right, self.left, far = (pos + 1) % 4, (pos + 3) % 4, (pos + 2) % 4
        self.a = copies.make(x.at[far, 0], first.at[0], plus)
        self.b = copies.make(x.at[far, 1], first.at[1], minus)
        self.c = copies.make(x.at[self.right], second.at[0], plus)
        self.d = copies.make(x.at[self.left], second.at[1], minus)

    def start(self):
        self.a.start()
        self.b.start()

    def middle(self):
        self.a.wait_recv()
        self.add(self.x.at[self.right, 0], self.x.at[self.right, 0], self.first.at[0])
        self.c.start()
        self.b.wait_recv()
        self.add(self.x.at[self.left, 1], self.x.at[self.left, 1], self.first.at[1])
        self.d.start()

    def arrived(self):
        self.c.wait_recv()
        self.d.wait_recv()

    def drain(self):
        for copy in (self.a, self.b, self.c, self.d):
            copy.wait_send()


class Gather:
    def __init__(self, copies, x, pos, plus, minus, own=None):
        source = x.at[pos] if own is None else own
        right, left = (pos + 1) % 4, (pos + 3) % 4
        self.a = copies.make(source, x.at[pos], plus)
        self.b = copies.make(source, x.at[pos], minus)
        self.c = copies.make(x.at[left, 0], x.at[left, 0], plus)
        self.d = copies.make(x.at[right, 1], x.at[right, 1], minus)

    def start(self):
        self.a.start()
        self.b.start()

    def middle(self):
        self.a.wait_recv()
        self.c.start()
        self.b.wait_recv()
        self.d.start()

    def arrived(self):
        self.c.wait_recv()
        self.d.wait_recv()

    def drain(self):
        for copy in (self.a, self.b, self.c, self.d):
            copy.wait_send()


def greet(near):
    barrier = pltpu.get_barrier_semaphore()
    for device in near:
        pl.semaphore_signal(barrier, inc=1, device_id=device, device_id_type=MESH)
    pl.semaphore_wait(barrier, len(near))


def add_rows(count, step):
    def add(dst, a, b):
        def body(i, _):
            at = pl.ds(pl.multiple_of(i * step, step), step)
            dst[at, :] = a[at, :] + b[at, :]
            return 0

        lax.fori_loop(0, count // step, body, 0)

    return add


def add_tiles(dst, a, b):
    if len(dst.shape) == 2:
        dst[...] = a[...] + b[...]
        return

    def body(i, _):
        add_tiles(dst.at[i], a.at[i], b.at[i])
        return 0

    lax.fori_loop(0, dst.shape[0], body, 0)


def select_kernel(blocks, parent, out):
    leaf, _, core, row, _, _, z = place()
    owner = leaf * 8 + row
    step = pl.program_id(0)
    kind, y_to = step // 4, step % 4
    parity = jnp.where(kind == 0, core, 1 - core)

    def body(n, _):
        h_to, xl_to, j = n // 16, (n // 8) % 2, n % 8
        child = 2 * xl_to + parity
        r = blocks[child, 4 * h_to + y_to] - 4 * owner
        c = blocks[child, j] - 32 * z
        held = (r >= 0) & (r < 4) & (c >= 0) & (c < 32)
        r, c = jnp.clip(r, 0, 3), jnp.clip(c, 0, 31)
        tile = parent[pl.ds(pl.multiple_of(r * BLK, BLK), BLK), pl.ds(pl.multiple_of(c * BLK, BLK), BLK)]
        out[0, 0, n] = jnp.where(held, tile, 0.0)
        return 0

    lax.fori_loop(0, 32, body, 0)


def select(child_map, parent):
    return pl.pallas_call(
        select_kernel,
        grid=(8,),
        out_shape=jax.ShapeDtypeStruct((2, 4, 32, BLK, BLK), F32),
        in_specs=[
            pl.BlockSpec(memory_space=pltpu.SMEM),
            pl.BlockSpec(parent.shape, lambda s: (0, 0), pipeline_mode=pl.Buffered(1)),
        ],
        out_specs=pl.BlockSpec((1, 1, 32, BLK, BLK), lambda s: (s // 4, s % 4, 0, 0, 0)),
        compiler_params=pltpu.CompilerParams(vmem_limit_bytes=32 << 20),
        name="select",
    )(child_map, parent)


CHUNKS = 4


def front_kernel(
    inverse, lower, tiles,
    strips, right, mate, update, off,
    lower_all, high, low, xf, f1, f2, fx, fpair, fall,
    sib, xp, p1, p2, xq, q1, q2, xr, r1, r2, uown, uall, upair, ucat,
    send, recv, local,
):
    leaf, xl, core, row, h, y, z = place()
    near = neighbours()
    copies = Copies(send, recv)
    role = (z + 2 * h) % 4
    slot = ((role + 1) // 2) % 2
    even = z % 2 == 0
    pair = (leaf, row, jnp.where(even, (z + 1) % 4, (z + 3) % 4))
    cross = (leaf, row, jnp.where(even, (z + 3) % 4, (z + 1) % 4))
    source, upper = role < 2, h == 0
    top = source & upper
    depth, width = inverse.shape
    piece = depth // CHUNKS

    lower_gather = Gather(copies, lower_all, z, near["zp"], near["zm"], own=lower)
    to_sibling = [copies.make(tiles.at[1, (y + d) % 4], sib.at[(y + d) % 4], near["core"]) for d in (2, 1, 3, 0)]
    to_top = []
    for q in range(CHUNKS):
        at = pl.ds(q * piece, piece)
        to_top.append(copies.make(inverse.at[at], right.at[at], near["hx"]))
    swap = copies.make(inverse, mate, pair)
    rs_f = Scatter(copies, xf, f1, f2, y, near["yp"], near["ym"], add_rows(BLK, 32))
    rs_p = Scatter(copies, xp, p1, p2, y, near["yp"], near["ym"], add_tiles)
    rs_q = Scatter(copies, xq, q1, q2, 2 * h + xl, near["xp"], near["xm"], add_tiles)
    rs_r = Scatter(copies, xr, r1, r2, z, near["zp"], near["zm"], add_tiles)
    ag_f = Gather(copies, fall, y, near["yp"], near["ym"])
    ag_u = Gather(copies, uall, z, near["zp"], near["zm"])
    f_out = copies.make(fpair.at[1 - h], fx, near["hx"])
    f_back = copies.make(fall.at[y, h], fall.at[y, h], near["hx"])
    u_swap = copies.make(uall, upair, near["hx"])

    def spread(src, at_src, at):
        return (
            copies.make(src.at[at_src], strips.at[slot, at], cross),
            copies.make(src.at[at_src], strips.at[slot, at], pair),
            copies.make(strips.at[slot, at], strips.at[slot, at], pair),
        )

    spread_a = [spread(right, pl.ds(q * piece, piece), pl.ds(q * piece, piece)) for q in range(CHUNKS)]
    spread_f = [spread(fall.at[y, k], slice(None), pl.ds(depth + k * BLK, BLK)) for k in range(2)]

    def spread_start(s):
        s[0].start()
        s[1].start()

    def spread_forward(s):
        s[0].wait_recv()
        s[2].start()

    greet(list(near.values()))

    lower_here = pltpu.make_async_copy(lower, lower_all.at[z], local.at[0])
    lower_here.start()
    lower_gather.start()
    tiles_here = []
    for n, d in enumerate((2, 1, 3, 0)):
        to_sibling[n].start()
        copy = pltpu.make_async_copy(tiles.at[0, (y + d) % 4], xp.at[(y + d) % 4], local.at[1 + n])
        copy.start()
        tiles_here.append(copy)
    inverse_here = pltpu.make_async_copy(inverse, right.at[pl.ds(0, depth)], local.at[5])

    @pl.when(h == 1)
    def _():
        for copy in to_top:
            copy.start()
        inverse_here.start()

    @pl.when(top)
    def _():
        swap.start()

    def split_rows(i, _):
        at = pl.ds(pl.multiple_of(i * 32, 32), 32)
        high[at, :], low[at, :] = split(inverse[at, :])
        return 0

    lax.fori_loop(0, depth // 32, split_rows, 0)

    def sum_tiles(n):
        d = (2, 1, 3, 0)[n]
        tiles_here[n].wait()
        to_sibling[n].wait_recv()
        add_tiles(xp.at[(y + d) % 4], xp.at[(y + d) % 4], sib.at[(y + d) % 4])

    lower_gather.middle()
    sum_tiles(0)
    rs_p.start()
    lower_here.wait()
    lower_gather.arrived()

    def factor_rows(k, _):
        block = jnp.concatenate([lower_all[k, 0], lower_all[k, 1]], axis=0)
        a_high, a_low = split(block)
        product = dot3(a_high, a_low, high[...], low[...])
        xf[2 * (k % 2), k // 2] = product[:BLK]
        xf[2 * (k % 2) + 1, k // 2] = product[BLK:]
        return 0

    lax.fori_loop(0, 4, factor_rows, 0)
    rs_f.start()
    for n in (1, 2, 3):
        sum_tiles(n)
    rs_f.middle()
    rs_p.middle()

    @pl.when(h == 1)
    def _():
        inverse_here.wait()

    for q in range(CHUNKS):

        @pl.when(upper)
        def _(q=q):
            to_top[q].wait_recv()

        @pl.when(source)
        def _(q=q):
            spread_start(spread_a[q])

    rs_f.arrived()
    for k in range(2):
        add_rows(BLK, 32)(fpair.at[k], xf.at[y, k], f2.at[0, k])
        add_rows(BLK, 32)(fpair.at[k], fpair.at[k], f2.at[1, k])
    f_out.start()

    @pl.when(jnp.logical_not(source))
    def _():
        for s in spread_a:
            spread_forward(s)

    f_out.wait_recv()
    add_rows(BLK, 32)(fall.at[y, h], fpair.at[h], fx)
    f_back.start()
    f_back.wait_recv()
    ag_f.start()

    @pl.when(source)
    def _():
        for s in spread_f:
            spread_start(s)

    rs_p.arrived()
    for k in range(2):
        for x in range(2):
            for g in range(2):
                add_tiles(xq.at[2 * k + x, g], xp.at[y, k, x, g], p2.at[0, k, x, g])
                add_tiles(xq.at[2 * k + x, g], xq.at[2 * k + x, g], p2.at[1, k, x, g])
    rs_q.start()

    @pl.when(jnp.logical_not(source))
    def _():
        for s in spread_f:
            spread_forward(s)

    ag_f.middle()
    rs_q.middle()
    rs_q.arrived()
    here = 2 * h + xl
    for g in range(2):
        for k in range(4):
            xr[2 * g + k // 2, k % 2] = xq[here, g, k] + q2[0, g, k] + q2[1, g, k]
    rs_r.start()
    rs_r.middle()
    rs_r.arrived()
    for k in range(2):
        tile = xr[z, k] + r2[0, k] + r2[1, k]
        uall[z, k] = tile
        update[:, k * BLK : (k + 1) * BLK] = tile
    ag_u.start()
    ag_u.middle()
    ag_u.arrived()
    u_swap.start()
    u_swap.wait_recv()
    ag_f.arrived()
    for j in range(8):
        to = (2 * (j % 4) + j // 4) * BLK
        ucat[pl.ds(pl.multiple_of(h * BLK, BLK), BLK), to : to + BLK] = uall[j // 2, j % 2]
        ucat[pl.ds(pl.multiple_of((1 - h) * BLK, BLK), BLK), to : to + BLK] = upair[j // 2, j % 2]

    u_high, u_low = split(ucat[...])
    total = jnp.zeros((2 * BLK, width), F32)
    for k in range(4):
        f_high, f_low = split(jnp.concatenate([fall[k, 0], fall[k, 1]], axis=0))
        at = slice(2 * k * BLK, 2 * (k + 1) * BLK)
        total = total + dot3(u_high[:, at], u_low[:, at], f_high, f_low)
    right[pl.ds(depth, 2 * BLK), :] = total
    off[...] = -2.0 * right[pl.ds(pl.multiple_of(depth + h * BLK, BLK), BLK), :]

    own = pltpu.make_async_copy(right.at[pl.ds(0, depth)], strips.at[slot, pl.ds(0, depth)], local.at[6])
    own_f = [
        pltpu.make_async_copy(fall.at[y, k], strips.at[slot, pl.ds(depth + k * BLK, BLK)], local.at[7 + k]) for k in range(2)
    ]

    @pl.when(source)
    def _():
        own.start()
        for copy in own_f:
            copy.start()
        own.wait()
        for copy in own_f:
            copy.wait()

    for s in spread_a + spread_f:

        @pl.when(source)
        def _(s=s):
            s[1].wait_recv()
            s[0].wait_send()
            s[1].wait_send()

        @pl.when(jnp.logical_not(source))
        def _(s=s):
            s[2].wait_recv()
            s[2].wait_send()

    @pl.when(top)
    def _():
        swap.wait()

    @pl.when(h == 1)
    def _():
        for copy in to_top:
            copy.wait_send()

    for copy in to_sibling + [f_out, f_back, u_swap]:
        copy.wait_send()
    for group in (lower_gather, rs_f, rs_p, rs_q, rs_r, ag_f, ag_u):
        group.drain()


def front(inverse, lower, tiles):
    depth, width = inverse.shape
    tall = depth + 2 * BLK
    vmem = lambda *shape: pltpu.VMEM(shape, F32)
    tile = (BLK, BLK)
    rows = (BLK, width)
    scratch = [
        vmem(4, 2, BLK, depth),
        pltpu.VMEM((depth, width), BF16),
        pltpu.VMEM((depth, width), BF16),
        vmem(4, 2, *rows),
        vmem(2, *rows),
        vmem(2, 2, *rows),
        vmem(*rows),
        vmem(2, *rows),
        vmem(4, 2, *rows),
        vmem(4, 2, 2, 2, 4, *tile),
        vmem(4, 2, 2, 2, 4, *tile),
        vmem(2, 2, 2, 4, *tile),
        vmem(2, 2, 2, 2, 4, *tile),
        vmem(4, 2, 4, *tile),
        vmem(2, 4, *tile),
        vmem(2, 2, 4, *tile),
        vmem(4, 2, *tile),
        vmem(2, *tile),
        vmem(2, 2, *tile),
        vmem(*tile),
        vmem(4, 2, *tile),
        vmem(4, 2, *tile),
        vmem(2 * BLK, 8 * BLK),
        pltpu.SemaphoreType.DMA((64,)),
        pltpu.SemaphoreType.DMA((64,)),
        pltpu.SemaphoreType.DMA((16,)),
    ]
    whole = pl.BlockSpec(memory_space=pltpu.VMEM)
    return pl.pallas_call(
        front_kernel,
        out_shape=(
            jax.ShapeDtypeStruct((2, tall, width), F32),
            jax.ShapeDtypeStruct((tall, width), F32),
            jax.ShapeDtypeStruct((depth, width), F32),
            jax.ShapeDtypeStruct((BLK, 2 * BLK), F32),
            jax.ShapeDtypeStruct((BLK, width), F32),
        ),
        in_specs=[whole, whole, pl.BlockSpec(memory_space=pl.ANY)],
        out_specs=(whole,) * 5,
        scratch_shapes=scratch,
        compiler_params=pltpu.CompilerParams(collective_id=0, has_side_effects=True, vmem_limit_bytes=67043328),
        name="front",
    )(inverse, lower.reshape(2, BLK, depth), tiles.reshape(2, 4, 2, 2, 2, 4, *tile))


def pivot_kernel(part, out, first, second, send, recv):
    _, _, _, _, _, y, _ = place()
    near = neighbours()
    ring = (near["yp"], near["ym"])
    rows = part.shape[2]
    rs = Scatter(Copies(send, recv), part, first, second, y, *ring, add_rows(rows, 32))
    greet(list(ring))
    rs.start()
    rs.middle()
    rs.arrived()
    for k in range(2):

        def body(i, _, k=k):
            at = pl.ds(pl.multiple_of(i * 32, 32), 32)
            to = pl.ds(pl.multiple_of(i * 32 + k * rows, 32), 32)
            out[to, :] = part[y, k, at, :] + second[0, k, at, :] + second[1, k, at, :]
            return 0

        lax.fori_loop(0, rows // 32, body, 0)
    rs.drain()


def pivot_sum(part):
    _, _, rows, width = part.shape
    whole = pl.BlockSpec(memory_space=pltpu.VMEM)
    return pl.pallas_call(
        pivot_kernel,
        out_shape=jax.ShapeDtypeStruct((2 * rows, width), F32),
        in_specs=[whole],
        out_specs=whole,
        scratch_shapes=[
            pltpu.VMEM((2, rows, width), F32),
            pltpu.VMEM((2, 2, rows, width), F32),
            pltpu.SemaphoreType.DMA((4,)),
            pltpu.SemaphoreType.DMA((4,)),
        ],
        compiler_params=pltpu.CompilerParams(collective_id=1, has_side_effects=True, vmem_limit_bytes=40 << 20),
        name="pivot_sum",
    )(part)


def shards(parent_adj, child_map, lower_panel, pivot_inverse):
    inverse, lower = pivot_inverse[0], lower_panel[0]
    tiles = select(child_map, parent_adj)
    strips, right, mate, update, off = front(inverse, lower, tiles)
    high = lax.Precision.HIGH
    product = lambda w, v: jnp.einsum("skn,km->snm", w, v, precision=high, preferred_element_type=F32)
    part = product(strips, right)
    _, _, _, row, h, _, z = place()

    def with_top(part):
        first = jnp.where(z == 0, inverse, mate)
        last = jnp.where(z == 0, mate, inverse)
        return part + product(jnp.stack([first, last]), inverse)

    part = lax.cond((h == 0) & (z < 2), with_top, lambda part: part, part)
    width = part.shape[2]
    pivot = pivot_sum(part.reshape(4, 2, width // 4, width))
    return (update[None], off[None], pivot[None])


def solution(mesh):
    in_specs = (P(("leaf", "row"), "col"), P(), P("leaf", "col", "row"), P("leaf", "row", "col"))
    out_specs = (P("leaf", "row", "col"), P("leaf", "row", "col"), P("leaf", "row", "col"))
    return jax.shard_map(shards, mesh=mesh, in_specs=in_specs, out_specs=out_specs, check_vma=False)
```

time: 791 us -> 343 us (0.43)
  waiting for transfers between devices: 635 us -> 0 us
  Pallas kernels: 0 us -> 301 us
  matrix products: 64 us -> 26.3 us
  local copies, waits for them, and re-layouts: 44.8 us -> 11.6 us
  blocking collectives: 14.5 us -> 0 us
  other arithmetic: 16.4 us -> 2.73 us
  between operations: 14.2 us -> 0.7 us
    reduce_scatter x4 -> x0, waiting for transfers between devices: 461 us -> none  [the longest x1 192 us: shards(): lax.psum_scatter(first + second, 'row', scatter_dimension=0, tiled=True)]
    pallas_call x0 -> x3, Pallas kernels: none -> 301 us  [the longest x1 220 us: front(): pl.pallas_call(front_kernel, out_shape=(jax.ShapeDtypeStruct((2, tall, wi...]
    all_gather x4 -> x0, waiting for transfers between devices: 171 us -> none  [the longest x1 82.7 us: shards(): lax.all_gather(inverse, 'col', axis=1, tiled=True)]
    dot_general x4 -> x2, matrix products: 64 us -> 26.3 us  [shards(): jnp.einsum('skn,km->snm', w, v, precision=high, preferred_element_type=F32)]
    gather x4 -> x0, local copies, waits for them, and re-layouts: 19.6 us -> none  [the longest x2 16.8 us: shards(): picked = jnp.take(parent_view, column_safe.reshape(-1), axis=1)]
    all_gather x1 -> x0, blocking collectives: 14.5 us -> none  [shards(): update_all = lax.all_gather(update, 'col', axis=1, tiled=True)]
    select_n x3 -> x0, other arithmetic: 14.2 us -> none  [the longest x1 7.44 us: shards(): picked = jnp.where(column_owned[None, :, :, :, None], picked, 0.0)]
    reshape x4 -> x0, local copies, waits for them, and re-layouts: 13.9 us -> none  [the longest x1 9.05 us: shards(): parent_view = parent_adj.reshape(local_rows, column_blocks, BLK)]
  transfers between devices with their start and end apart: 8 -> 0, of which waited for: 7 -> 0; matrix products, arithmetic and copies ran while one was open for 13% -> 0% of each run, Pallas kernels for 0% -> 0%
where the time goes in v1:
time: 343 us
  Pallas kernels  301 us (88%)
  matrix products  26.3 us (8%)
  local copies, waits for them, and re-layouts  11.6 us (3%)
    pallas_call x1, Pallas kernels, front(): pl.pallas_call(front_kernel, out_shape=(jax.ShapeDtypeStruct((2, tall, wi...  220 us
    pallas_call x1, Pallas kernels, pivot_sum(): pl.pallas_call(pivot_kernel, out_shape=jax.ShapeDtypeStruct((2 * rows, wi...  69.1 us
    dot_general x2, matrix products, shards(): jnp.einsum('skn,km->snm', w, v, precision=high, preferred_element_type=F32)  26.3 us
    pallas_call x1, Pallas kernels, select(): pl.pallas_call(select_kernel, grid=(8,), out_shape=jax.ShapeDtypeStruct((...  12.2 us

profile of v1, /device:TPU:32, one launch (start us, length us, event | category | flops | bytes accessed | tf_op | source)
XLA Modules:
  0.0 342.5 jit_solution(11935497237189456710)
XLA Ops:
  0.6 0.0 copy-start
  0.6 3.4 copy-done
  4.0 0.0 copy-start.1
  4.0 0.7 copy-done.1
  4.7 12.2 %select.5 = f32[2,4,32,128,128]{4,3,2,1,0:T(8,128)} custom-call(s32[4,8]{1,0:T(4,128)S(1)} %copy-done.1, f32[512,4096]{1,0:T(8,128)S(1)} %copy-done), custom_call_target="tpu_custom_call" | custom-call | tf_op jit(solution)/shard_map/select/pallas_call | solution.py:166
  16.9 219.9 %front.1 = (f32[2,768,1024]{2,1,0:T(8,128)}, f32[768,1024]{1,0:T(8,128)}, f32[512,1024]{1,0:T(8,128)}, f32[128,256]{1,0:T(8,128)}, f32[128,1024]{1,0:T(8,128)}) custom-call(f32[512,1024]{1,0:T(8,128)} %bitcast.20, f32[2,128,512]{2,1,0:T(8,128)} %bitcast.22, f32[2,4,2,2,2,4,128,128]{7,6,5,4,3,2,1,0:T(8,128)} %bitcast.19), custom_call_target="tpu_custom_call" | custom-call | tf_op jit(solution)/shard_map/front/pallas_call | solution.py:455
  236.9 0.0 copy-start.2
  236.9 15.3 %fusion.9 = f32[2,1024,1024]{2,1,0:T(8,128)} fusion(f32[2,768,1024]{2,1,0:T(8,128)} %get-tuple-element.26, f32[768,1024]{1,0:T(8,128)} %get-tuple-element.27), kind=kOutput, calls=%fused_computation.9 | convolution fusion | flops 9663676416 | bytes 17825792 | tf_op jit(solution)/shard_map/skn,km->snm/dot_general | solution.py:518
  252.2 0.0 copy-done.2
  252.2 18.4 %conditional.1 = (f32[2,1024,1024]{2,1,0:T(8,128)}) conditional(s32[]{:T(128)} %convert_element_type.3, f32[2,1024,1024]{2,1,0:T(8,128)} %fusion.9, (s32[]{:T(128)}, f32[512,1024]{1,0:T(8,128)S(1)}, f32[512,1024]{1,0:T(8,128)}, f32[2,1024,1024]{2,1,0:T(8,128)}) %tuple.22), branch_computations={%region_0.1_spmd, %region_1.2_spmd} | conditional | flops 6446645248 | bytes 39845904 | solution.py:527
  252.2 1.8 copy.9
  254.0 2.9 copy.10
  257.0 2.7 select_bitcast_fusion.1
  259.7 11.0 %fusion.4 = f32[2,1024,1024]{2,1,0:T(8,128)} fusion(f32[2,1024,1024]{2,1,0:T(8,128)} %get-tuple-element.12, f32[1,512,1024]{1,2,0:T(8,128)S(1)} %get-tuple-element.34, f32[1,512,1024]{1,2,0:T(8,128)S(1)} %get-tuple-element.33, f32[512,1024]{1,0:T(8,128)S(1)} %get-tuple-element.30), kind=kOutput, calls=%fused_computation.4 | convolution fusion | flops 6445596672 | bytes 23068672 | tf_op jit(solution)/shard_map/cond/branch_1_fun/skn,km->snm/dot_general | solution.py:518
  270.7 0.0 copy-start.4
  270.7 0.0 copy-start.3
  270.7 69.1 %pivot_sum.1 = f32[512,1024]{1,0:T(8,128)S(1)} custom-call(f32[4,2,256,1024]{3,2,1,0:T(8,128)} %bitcast.9.part), custom_call_target="tpu_custom_call" | custom-call | tf_op jit(solution)/shard_map/pivot_sum/pallas_call | solution.py:497
  339.7 0.0 copy-done.4
  339.7 0.7 copy.17
  340.4 0.0 copy-done.3
  340.4 0.8 copy.18
  341.2 1.3 copy.19
Async XLA Ops:
  0.6 3.4 copy-start
  4.0 0.7 copy-start.1
  236.9 15.4 %copy-start.2 = (f32[1,512,1024]{2,1,0:T(8,128)S(1)}, f32[1,512,1024]{2,1,0:T(8,128)}, u32[]{:S(2)}) copy-start(f32[1,512,1024]{2,1,0:T(8,128)} %param.9) | copy-start | bytes 6291460
  270.7 69.1 %copy-start.4 = (f32[128,256]{1,0:T(8,128)S(1)}, f32[128,256]{1,0:T(8,128)}, u32[]{:S(2)}) copy-start(f32[128,256]{1,0:T(8,128)} %get-tuple-element.24) | copy-start | bytes 393220
  270.7 69.7 %copy-start.3 = (f32[128,1024]{1,0:T(8,128)S(1)}, f32[128,1024]{1,0:T(8,128)}, u32[]{:S(2)}) copy-start(f32[128,1024]{1,0:T(8,128)} %get-tuple-element.25) | copy-start | bytes 1572868

commit v2 on v1

--- a/solution.py
+++ b/solution.py
@@ -145,11 +145,12 @@
     leaf, _, core, row, _, _, z = place()
     owner = leaf * 8 + row
     step = pl.program_id(0)
-    kind, y_to = step // 4, step % 4
+    kind, x_to = step // 4, step % 4
+    h_to, xl_to = x_to // 2, x_to % 2
     parity = jnp.where(kind == 0, core, 1 - core)
 
     def body(n, _):
-        h_to, xl_to, j = n // 16, (n // 8) % 2, n % 8
+        y_to, j = n // 8, n % 8
         child = 2 * xl_to + parity
         r = blocks[child, 4 * h_to + y_to] - 4 * owner
         c = blocks[child, j] - 32 * z
@@ -190,6 +191,7 @@
     leaf, xl, core, row, h, y, z = place()
     near = neighbours()
     copies = Copies(send, recv)
+    here = 2 * h + xl
     role = (z + 2 * h) % 4
     slot = ((role + 1) // 2) % 2
     even = z % 2 == 0
@@ -201,15 +203,15 @@
     piece = depth // CHUNKS
 
     lower_gather = Gather(copies, lower_all, z, near["zp"], near["zm"], own=lower)
-    to_sibling = [copies.make(tiles.at[1, (y + d) % 4], sib.at[(y + d) % 4], near["core"]) for d in (2, 1, 3, 0)]
+    to_sibling = [copies.make(tiles.at[1, (here + d) % 4], sib.at[(here + d) % 4], near["core"]) for d in (2, 1, 3, 0)]
     to_top = []
     for q in range(CHUNKS):
         at = pl.ds(q * piece, piece)
         to_top.append(copies.make(inverse.at[at], right.at[at], near["hx"]))
     swap = copies.make(inverse, mate, pair)
     rs_f = Scatter(copies, xf, f1, f2, y, near["yp"], near["ym"], add_rows(BLK, 32))
-    rs_p = Scatter(copies, xp, p1, p2, y, near["yp"], near["ym"], add_tiles)
-    rs_q = Scatter(copies, xq, q1, q2, 2 * h + xl, near["xp"], near["xm"], add_tiles)
+    rs_p = Scatter(copies, xp, p1, p2, here, near["xp"], near["xm"], add_tiles)
+    rs_q = Scatter(copies, xq, q1, q2, y, near["yp"], near["ym"], add_tiles)
     rs_r = Scatter(copies, xr, r1, r2, z, near["zp"], near["zm"], add_tiles)
     ag_f = Gather(copies, fall, y, near["yp"], near["ym"])
     ag_u = Gather(copies, uall, z, near["zp"], near["zm"])
@@ -243,15 +245,13 @@
     tiles_here = []
     for n, d in enumerate((2, 1, 3, 0)):
         to_sibling[n].start()
-        copy = pltpu.make_async_copy(tiles.at[0, (y + d) % 4], xp.at[(y + d) % 4], local.at[1 + n])
+        copy = pltpu.make_async_copy(tiles.at[0, (here + d) % 4], xp.at[(here + d) % 4], local.at[1 + n])
         copy.start()
         tiles_here.append(copy)
     inverse_here = pltpu.make_async_copy(inverse, right.at[pl.ds(0, depth)], local.at[5])
 
     @pl.when(h == 1)
     def _():
-        for copy in to_top:
-            copy.start()
         inverse_here.start()
 
     @pl.when(top)
@@ -269,13 +269,22 @@
         d = (2, 1, 3, 0)[n]
         tiles_here[n].wait()
         to_sibling[n].wait_recv()
-        add_tiles(xp.at[(y + d) % 4], xp.at[(y + d) % 4], sib.at[(y + d) % 4])
-
-    lower_gather.middle()
+        add_tiles(xp.at[(here + d) % 4], xp.at[(here + d) % 4], sib.at[(here + d) % 4])
+
     sum_tiles(0)
     rs_p.start()
+    lower_gather.middle()
     lower_here.wait()
     lower_gather.arrived()
+
+    @pl.when(h == 1)
+    def _():
+        inverse_here.wait()
+
+    @pl.when(source & (h == 1))
+    def _():
+        for s in spread_a:
+            spread_start(s)
 
     def factor_rows(k, _):
         block = jnp.concatenate([lower_all[k, 0], lower_all[k, 1]], axis=0)
@@ -289,37 +298,35 @@
     rs_f.start()
     for n in (1, 2, 3):
         sum_tiles(n)
+    rs_p.middle()
+
+    @pl.when(h == 1)
+    def _():
+        for copy in to_top:
+            copy.start()
+
     rs_f.middle()
-    rs_p.middle()
-
-    @pl.when(h == 1)
-    def _():
-        inverse_here.wait()
-
-    for q in range(CHUNKS):
-
-        @pl.when(upper)
-        def _(q=q):
-            to_top[q].wait_recv()
-
-        @pl.when(source)
-        def _(q=q):
-            spread_start(spread_a[q])
-
+    rs_p.arrived()
+    for k in range(2):
+        for x in range(2):
+            for g in range(2):
+                add_tiles(xq.at[2 * k + x, g], xp.at[here, k, x, g], p2.at[0, k, x, g])
+                add_tiles(xq.at[2 * k + x, g], xq.at[2 * k + x, g], p2.at[1, k, x, g])
+    rs_q.start()
     rs_f.arrived()
     for k in range(2):
         add_rows(BLK, 32)(fpair.at[k], xf.at[y, k], f2.at[0, k])
         add_rows(BLK, 32)(fpair.at[k], fpair.at[k], f2.at[1, k])
     f_out.start()
-
-    @pl.when(jnp.logical_not(source))
-    def _():
-        for s in spread_a:
-            spread_forward(s)
-
+    rs_q.middle()
     f_out.wait_recv()
     add_rows(BLK, 32)(fall.at[y, h], fpair.at[h], fx)
     f_back.start()
+    rs_q.arrived()
+    for g in range(2):
+        for k in range(4):
+            xr[2 * g + k // 2, k % 2] = xq[y, g, k] + q2[0, g, k] + q2[1, g, k]
+    rs_r.start()
     f_back.wait_recv()
     ag_f.start()
 
@@ -328,35 +335,32 @@
         for s in spread_f:
             spread_start(s)
 
-    rs_p.arrived()
-    for k in range(2):
-        for x in range(2):
-            for g in range(2):
-                add_tiles(xq.at[2 * k + x, g], xp.at[y, k, x, g], p2.at[0, k, x, g])
-                add_tiles(xq.at[2 * k + x, g], xq.at[2 * k + x, g], p2.at[1, k, x, g])
-    rs_q.start()
-
-    @pl.when(jnp.logical_not(source))
-    def _():
-        for s in spread_f:
-            spread_forward(s)
-
-    ag_f.middle()
-    rs_q.middle()
-    rs_q.arrived()
-    here = 2 * h + xl
-    for g in range(2):
-        for k in range(4):
-            xr[2 * g + k // 2, k % 2] = xq[here, g, k] + q2[0, g, k] + q2[1, g, k]
-    rs_r.start()
     rs_r.middle()
+
+    for q in range(CHUNKS):
+
+        @pl.when(upper)
+        def _(q=q):
+            to_top[q].wait_recv()
+
+        @pl.when(source & upper)
+        def _(q=q):
+            spread_start(spread_a[q])
+
     rs_r.arrived()
     for k in range(2):
         tile = xr[z, k] + r2[0, k] + r2[1, k]
         uall[z, k] = tile
         update[:, k * BLK : (k + 1) * BLK] = tile
     ag_u.start()
+    ag_f.middle()
     ag_u.middle()
+
+    @pl.when(jnp.logical_not(source))
+    def _():
+        for s in spread_f + spread_a:
+            spread_forward(s)
+
     ag_u.arrived()
     u_swap.start()
     u_swap.wait_recv()

time: 343 us -> 409 us (1.19)
  the two profiles are of different devices: /device:TPU:32 before, /device:TPU:64 now
where the time goes in v2:
time: 409 us; the launch traced here: 408 us
  Pallas kernels  385 us (94%)
  matrix products  15.3 us (4%)
  local copies, waits for them, and re-layouts  6.84 us (2%)
    pallas_call x1, Pallas kernels, front(): pl.pallas_call(front_kernel, out_shape=(jax.ShapeDtypeStruct((2, tall, wi...  300 us
    pallas_call x1, Pallas kernels, pivot_sum(): pl.pallas_call(pivot_kernel, out_shape=jax.ShapeDtypeStruct((2 * rows, wi...  74.3 us
    dot_general x1, matrix products, shards(): jnp.einsum('skn,km->snm', w, v, precision=high, preferred_element_type=F32)  15.3 us
    pallas_call x1, Pallas kernels, select(): pl.pallas_call(select_kernel, grid=(8,), out_shape=jax.ShapeDtypeStruct((...  11.3 us

profile of v2, /device:TPU:64, one launch (start us, length us, event | category | flops | bytes accessed | tf_op | source)
XLA Modules:
  0.0 408.4 jit_solution(9863991042772002090)
XLA Ops:
  0.6 0.0 copy-start
  0.6 3.4 copy-done
  4.0 0.0 copy-start.1
  4.0 0.7 copy-done.1
  4.7 11.3 %select.5 = f32[2,4,32,128,128]{4,3,2,1,0:T(8,128)} custom-call(s32[4,8]{1,0:T(4,128)S(1)} %copy-done.1, f32[512,4096]{1,0:T(8,128)S(1)} %copy-done), custom_call_target="tpu_custom_call" | custom-call | tf_op jit(solution)/shard_map/select/pallas_call | solution.py:167
  16.0 299.8 %front.1 = (f32[2,768,1024]{2,1,0:T(8,128)}, f32[768,1024]{1,0:T(8,128)}, f32[512,1024]{1,0:T(8,128)}, f32[128,256]{1,0:T(8,128)}, f32[128,1024]{1,0:T(8,128)}) custom-call(f32[512,1024]{1,0:T(8,128)} %bitcast.20, f32[2,128,512]{2,1,0:T(8,128)} %bitcast.22, f32[2,4,2,2,2,4,128,128]{7,6,5,4,3,2,1,0:T(8,128)} %bitcast.19), custom_call_target="tpu_custom_call" | custom-call | tf_op jit(solution)/shard_map/front/pallas_call | solution.py:459
  315.9 0.0 copy-start.2
  315.9 15.3 %fusion.9 = f32[2,1024,1024]{2,1,0:T(8,128)} fusion(f32[2,768,1024]{2,1,0:T(8,128)} %get-tuple-element.26, f32[768,1024]{1,0:T(8,128)} %get-tuple-element.27), kind=kOutput, calls=%fused_computation.9 | convolution fusion | flops 9663676416 | bytes 17825792 | tf_op jit(solution)/shard_map/skn,km->snm/dot_general | solution.py:522
  331.2 0.0 copy-done.2
  331.2 0.0 copy-start.4
  331.2 0.0 copy-start.3
  331.2 74.3 %pivot_sum.1 = f32[512,1024]{1,0:T(8,128)S(1)} custom-call(f32[4,2,256,1024]{3,2,1,0:T(8,128)} %bitcast.9.part), custom_call_target="tpu_custom_call" | custom-call | tf_op jit(solution)/shard_map/pivot_sum/pallas_call | solution.py:501
  405.6 0.0 copy-done.4
  405.6 0.7 copy.17
  406.2 0.0 copy-done.3
  406.2 0.8 copy.18
  407.0 1.3 copy.19
  (1 shorter events, 0.0 us)
Async XLA Ops:
  0.6 3.4 copy-start
  4.0 0.7 copy-start.1
  315.9 15.4 %copy-start.2 = (f32[1,512,1024]{2,1,0:T(8,128)S(1)}, f32[1,512,1024]{2,1,0:T(8,128)}, u32[]{:S(2)}) copy-start(f32[1,512,1024]{2,1,0:T(8,128)} %param.9) | copy-start | bytes 6291460
  331.2 74.4 %copy-start.4 = (f32[128,256]{1,0:T(8,128)S(1)}, f32[128,256]{1,0:T(8,128)}, u32[]{:S(2)}) copy-start(f32[128,256]{1,0:T(8,128)} %get-tuple-element.24) | copy-start | bytes 393220
  331.2 75.0 %copy-start.3 = (f32[128,1024]{1,0:T(8,128)S(1)}, f32[128,1024]{1,0:T(8,128)}, u32[]{:S(2)}) copy-start(f32[128,1024]{1,0:T(8,128)} %get-tuple-element.25) | copy-start | bytes 1572868

commit v3 on v1

--- a/solution.py
+++ b/solution.py
@@ -182,9 +182,9 @@
 
 def front_kernel(
     inverse, lower, tiles,
-    strips, right, mate, update, off,
+    strips, right, mate, extra, update, off,
     lower_all, high, low, xf, f1, f2, fx, fpair, fall,
-    sib, xp, p1, p2, xq, q1, q2, xr, r1, r2, uown, uall, upair, ucat,
+    sib, xp, p1, p2, xq, q1, q2, xr, r1, r2, held, uall, upair, ucat,
     send, recv, local,
 ):
     leaf, xl, core, row, h, y, z = place()
@@ -305,6 +305,27 @@
         @pl.when(source)
         def _(q=q):
             spread_start(spread_a[q])
+
+    @pl.when(top)
+    def _():
+        swap.wait_recv()
+        cross_dot = lambda p, q: lax.dot_general(p, q, (((0,), (0,)), ((), ())), preferred_element_type=F32)
+
+        def body(n, _):
+            at = pl.ds(pl.multiple_of(n * 256, 256), 256)
+            m_high, m_low = split(mate[:, at])
+            for k, (to, w_high, w_low) in enumerate(((z, high[:, at], low[:, at]), (1 - z, m_high, m_low))):
+                out = pltpu.make_async_copy(held.at[k], extra.at[to, at], local.at[9 + k])
+
+                @pl.when(n > 0)
+                def _():
+                    out.wait()
+
+                held[k] = cross_dot(w_high, high[...]) + (cross_dot(w_high, low[...]) + cross_dot(w_low, high[...]))
+                out.start()
+            return 0
+
+        lax.fori_loop(0, width // 256, body, 0)
 
     rs_f.arrived()
     for k in range(2):
@@ -404,7 +425,9 @@
 
     @pl.when(top)
     def _():
-        swap.wait()
+        swap.wait_send()
+        for k in range(2):
+            pltpu.make_async_copy(held.at[k], extra.at[k, pl.ds(0, 256)], local.at[9 + k]).wait()
 
     @pl.when(h == 1)
     def _():
@@ -443,7 +466,7 @@
         vmem(4, 2, *tile),
         vmem(2, *tile),
         vmem(2, 2, *tile),
-        vmem(*tile),
+        vmem(2, 256, width),
         vmem(4, 2, *tile),
         vmem(4, 2, *tile),
         vmem(2 * BLK, 8 * BLK),
@@ -458,11 +481,12 @@
             jax.ShapeDtypeStruct((2, tall, width), F32),
             jax.ShapeDtypeStruct((tall, width), F32),
             jax.ShapeDtypeStruct((depth, width), F32),
+            jax.ShapeDtypeStruct((2, width, width), F32),
             jax.ShapeDtypeStruct((BLK, 2 * BLK), F32),
             jax.ShapeDtypeStruct((BLK, width), F32),
         ),
         in_specs=[whole, whole, pl.BlockSpec(memory_space=pl.ANY)],
-        out_specs=(whole,) * 5,
+        out_specs=(whole,) * 3 + (pl.BlockSpec(memory_space=pl.ANY),) + (whole,) * 2,
         scratch_shapes=scratch,
         compiler_params=pltpu.CompilerParams(collective_id=0, has_side_effects=True, vmem_limit_bytes=67043328),
         name="front",
@@ -513,18 +537,10 @@
 def shards(parent_adj, child_map, lower_panel, pivot_inverse):
     inverse, lower = pivot_inverse[0], lower_panel[0]
     tiles = select(child_map, parent_adj)
-    strips, right, mate, update, off = front(inverse, lower, tiles)
-    high = lax.Precision.HIGH
-    product = lambda w, v: jnp.einsum("skn,km->snm", w, v, precision=high, preferred_element_type=F32)
-    part = product(strips, right)
-    _, _, _, row, h, _, z = place()
-
-    def with_top(part):
-        first = jnp.where(z == 0, inverse, mate)
-        last = jnp.where(z == 0, mate, inverse)
-        return part + product(jnp.stack([first, last]), inverse)
-
-    part = lax.cond((h == 0) & (z < 2), with_top, lambda part: part, part)
+    strips, right, _, extra, update, off = front(inverse, lower, tiles)
+    part = jnp.einsum("skn,km->snm", strips, right, precision=lax.Precision.HIGH, preferred_element_type=F32)
+    _, _, _, _, h, _, z = place()
+    part = part + jnp.where((h == 0) & (z < 2), extra, 0.0)
     width = part.shape[2]
     pivot = pivot_sum(part.reshape(4, 2, width // 4, width))
     return (update[None], off[None], pivot[None])

time: 343 us -> 320 us (0.933)
  matrix products: 26.3 us -> 14.5 us
  local copies, waits for them, and re-layouts: 11.6 us -> 6.83 us
    dot_general x2 -> x1, matrix products: 26.3 us -> 14.5 us  [shards(): jnp.einsum('skn,km->snm', strips, right, precision=lax.Precision.HIGH, pr...]
    another operation x2 -> x0, local copies, waits for them, and re-layouts: 4.73 us -> none
where the time goes in v3:
time: 320 us
  Pallas kernels  298 us (93%)
  matrix products  14.5 us (5%)
  local copies, waits for them, and re-layouts  6.83 us (2%)
    pallas_call x1, Pallas kernels, front(): pl.pallas_call(front_kernel, out_shape=(jax.ShapeDtypeStruct((2, tall, wi...  220 us
    pallas_call x1, Pallas kernels, pivot_sum(): pl.pallas_call(pivot_kernel, out_shape=jax.ShapeDtypeStruct((2 * rows, wi...  65.8 us
    dot_general x1, matrix products, shards(): jnp.einsum('skn,km->snm', strips, right, precision=lax.Precision.HIGH, pr...  14.5 us
    pallas_call x1, Pallas kernels, select(): pl.pallas_call(select_kernel, grid=(8,), out_shape=jax.ShapeDtypeStruct((...  12.2 us
    unnamed x11, local copies, waits for them, and re-layouts  6.83 us

profile of v3, /device:TPU:32, one launch (start us, length us, event | category | flops | bytes accessed | tf_op | source)
XLA Modules:
  0.0 319.9 jit_solution(11117081427228552014)
XLA Ops:
  0.6 0.0 copy-start
  0.6 3.4 %copy-done = f32[512,4096]{1,0:T(8,128)S(1)} copy-done((f32[512,4096]{1,0:T(8,128)S(1)}, f32[512,4096]{1,0:T(8,128)}, u32[]{:S(2)}) %copy-start) | copy-done | bytes 8388632
  4.0 0.0 copy-start.1
  4.0 0.7 copy-done.1
  4.7 12.2 %select.5 = f32[2,4,32,128,128]{4,3,2,1,0:T(8,128)} custom-call(s32[4,8]{1,0:T(4,128)S(1)} %copy-done.1, f32[512,4096]{1,0:T(8,128)S(1)} %copy-done), custom_call_target="tpu_custom_call" | custom-call | tf_op jit(solution)/shard_map/select/pallas_call | solution.py:166
  16.9 219.9 %front.1 = (f32[2,768,1024]{2,1,0:T(8,128)}, f32[768,1024]{1,0:T(8,128)}, f32[512,1024]{1,0:T(8,128)}, f32[2,1024,1024]{2,1,0:T(8,128)}, f32[128,256]{1,0:T(8,128)}, /*index=5*/f32[128,1024]{1,0:T(8,128)}) custom-call(f32[512,1024]{1,0:T(8,128)} %bitcast.16, f32[2,128,512]{2,1,0:T(8,128)} %bitcast.17, f32[2,4,2,2,2,4,128,128]{7,6,5,4,3,2,1,0:T(8,128)} %bitcast.15), custom_call_target="tpu_custom_call" | custom-call | tf_op jit(solution)/shard_map/front/pallas_call | solution.py:478
  236.8 14.5 %select_add_fusion = f32[2,1024,1024]{2,1,0:T(8,128)S(1)} fusion(f32[2,1024,1024]{2,1,0:T(8,128)} %get-tuple-element.12, pred[]{:T(512)S(6)} %and.11, f32[2,768,1024]{2,1,0:T(8,128)} %get-tuple-element.10, f32[768,1024]{1,0:T(8,128)} %get-tuple-element.11), kind=kOutput, calls=%fused_computation | convolution fusion | flops 9667870720 | bytes 26214400 | tf_op jit(solution)/shard_map/skn,km->snm/dot_general | solution.py:541
  251.3 0.0 copy-start.3
  251.3 0.0 copy-start.2
  251.3 65.8 %pivot_sum.1 = f32[512,1024]{1,0:T(8,128)S(1)} custom-call(f32[4,2,256,1024]{3,2,1,0:T(8,128)S(1)} %bitcast.13), custom_call_target="tpu_custom_call" | custom-call | tf_op jit(solution)/shard_map/pivot_sum/pallas_call | solution.py:521
  317.1 0.0 copy-done.3
  317.1 0.7 copy.12
  317.7 0.0 copy-done.2
  317.7 0.8 copy.13
  318.5 1.3 copy.14
Async XLA Ops:
  0.6 3.4 %copy-start = (f32[512,4096]{1,0:T(8,128)S(1)}, f32[512,4096]{1,0:T(8,128)}, u32[]{:S(2)}) copy-start(f32[512,4096]{1,0:T(8,128)} %parent.1) | copy-start | bytes 25165828
  4.0 0.7 copy-start.1
  251.3 65.8 %copy-start.3 = (f32[128,256]{1,0:T(8,128)S(1)}, f32[128,256]{1,0:T(8,128)}, u32[]{:S(2)}) copy-start(f32[128,256]{1,0:T(8,128)} %get-tuple-element.8) | copy-start | bytes 393220
  251.3 66.5 %copy-start.2 = (f32[128,1024]{1,0:T(8,128)S(1)}, f32[128,1024]{1,0:T(8,128)}, u32[]{:S(2)}) copy-start(f32[128,1024]{1,0:T(8,128)} %get-tuple-element.9) | copy-start | bytes 1572868
